TPU v7x, 32 devices: a whole 2x2x4 slice. The times are simulated.
32 devices in a mesh: dp: 4 (over x, core), row: 4 (over z), col: 2 (over y).
Axes of the slice: x: 2, y: 2, z: 4, core: 2. Of those that a mesh axis runs over, the one named last changes fastest.
Arguments:
- hidden_in: float32 [1024, 32768], P('col', ('dp', 'row')), may hold values from -6 to 6
- lengths: int32 [64], P(('dp', 'row')), may hold values from 1 to 512, as said below
- ln1_gain: float32 [1024], P('col'), may hold values from 0.25 to 1.75
- ln1_shift: float32 [1024], P('col'), may hold values from -3 to 3
- w_qkv: bfloat16 [1024, 3072], P('row', 'col'), may hold values from -0.1875 to 0.1875
- bias_q: float32 [1024], P('col'), may hold values from -3 to 3
- bias_v: float32 [1024], P('col'), may hold values from -3 to 3
- w_out: bfloat16 [1024, 1024], P('col', 'row'), may hold values from -0.375 to 0.375
- bias_out: float32 [1024], P('col'), may hold values from -3 to 3
- ln2_gain: float32 [1024], P('col'), may hold values from 0.25 to 1.75
- ln2_shift: float32 [1024], P('col'), may hold values from -3 to 3
- w_up: bfloat16 [1024, 4096], P('row', 'col'), may hold values from -0.1875 to 0.1875
- bias_up: float32 [4096], P('col'), may hold values from -3 to 3
- w_down: bfloat16 [4096, 1024], P('col', 'row'), may hold values from -0.125 to 0.125
- bias_down: float32 [1024], P('col'), may hold values from -3 to 3
- cotangent: float32 [1024, 32768], P('col', ('dp', 'row')), may hold values from -6 to 6
Outputs:
- hidden_out: float32 [1024, 32768], P('col', ('dp', 'row'))
- grad_in: float32 [1024, 32768], P('col', ('dp', 'row'))
- grad_ln1_gain: float32 [1024], P('col')
- grad_ln1_shift: float32 [1024], P('col')
- grad_w_qkv: float32 [1024, 3072], P('row', 'col')
- grad_bias_q: float32 [1024], P('col')
- grad_bias_v: float32 [1024], P('col')
- grad_w_out: float32 [1024, 1024], P('col', 'row')
- grad_bias_out: float32 [1024], P('col')
- grad_ln2_gain: float32 [1024], P('col')
- grad_ln2_shift: float32 [1024], P('col')
- grad_w_up: float32 [1024, 4096], P('row', 'col')
- grad_bias_up: float32 [4096], P('col')
- grad_w_down: float32 [4096, 1024], P('col', 'row')
- grad_bias_down: float32 [1024], P('col')
Inputs may be any that keep to these rules, and one draw needn't show every extreme that they name: `lengths`: each slot holds one sequence of this many tokens followed by padding; some slot of every index pair of dp and row is full.
All inputs are finite; a program needn't handle non-finite values.
Results may differ from a plain program's by a relative error of at most 0.019.
Values may be sent and summed in bfloat16 or wider, within the bound.
A program may use at most 192 MiB of HBM per device.

v0:
```python
from functools import partial
import jax
import jax.numpy as jnp
from jax import lax
from jax.sharding import PartitionSpec as P

HEADS = 16
HEAD = 64
EPS = 1e-05
NEG = -1e30


def norm_forward(value, gain, shift):
    width = value.shape[1] * lax.axis_size("col")
    sums = lax.psum((jnp.sum(value, axis=1), jnp.sum(value * value, axis=1)), "col")
    mean = (sums[0] / width)[:, None]
    var = (sums[1] / width)[:, None] - mean * mean
    inverse = lax.rsqrt(var + EPS)
    normed = (value - mean) * inverse
    return (normed, inverse, (normed * gain + shift).astype(jnp.bfloat16))


def norm_backward(incoming, normed, inverse, gain):
    width = incoming.shape[1] * lax.axis_size("col")
    scaled = incoming * gain
    sums = lax.psum((jnp.sum(scaled, axis=1), jnp.sum(scaled * normed, axis=1)), "col")
    return inverse * (scaled - sums[0][:, None] / width - normed * sums[1][:, None] / width)


def gather_rows(value):
    return lax.all_gather(value, "col", axis=1, tiled=True)


def back_columns(value):
    return lax.psum_scatter(
        value.astype(jnp.bfloat16), "col", scatter_dimension=1, tiled=True
    ).astype(jnp.float32)


def slot_scores(slopes, query, keys, length):
    span = query.shape[0]
    pos = jnp.arange(span)
    offset = (pos[None, :] - pos[:, None]).astype(jnp.float32)
    raw = jnp.einsum("qhd,khd->hqk", query, keys, preferred_element_type=jnp.float32) * 0.125
    raw = raw + slopes[:, None, None] * offset[None]
    visible = (pos[None, :] <= pos[:, None]) & (pos[None, :] < length)
    return jnp.where(visible[None], raw, NEG)


def forward_slot(slopes, item):
    query, keys, values, length = item
    scores = slot_scores(slopes, query, keys, length)
    top = jnp.max(scores, axis=-1, keepdims=True)
    expo = jnp.exp(scores - top)
    total = jnp.sum(expo, axis=-1, keepdims=True)
    probs = expo / total
    attended = jnp.einsum(
        "hqk,khd->qhd", probs.astype(jnp.bfloat16), values, preferred_element_type=jnp.float32
    )
    return (attended, (top + jnp.log(total))[..., 0])


def backward_slot(slopes, item):
    query, keys, values, grad_out, lse, length = item
    scores = slot_scores(slopes, query, keys, length)
    probs = jnp.exp(scores - lse[..., None])
    grad_probs = jnp.einsum("qhd,khd->hqk", grad_out, values, preferred_element_type=jnp.float32)
    grad_values = jnp.einsum(
        "hqk,qhd->khd", probs.astype(jnp.bfloat16), grad_out, preferred_element_type=jnp.float32
    )
    inner = jnp.sum(probs * grad_probs, axis=-1, keepdims=True)
    grad_scores = (probs * (grad_probs - inner)).astype(jnp.bfloat16)
    grad_query = (
        jnp.einsum("hqk,khd->qhd", grad_scores, keys, preferred_element_type=jnp.float32) * 0.125
    )
    grad_keys = (
        jnp.einsum("hqk,qhd->khd", grad_scores, query, preferred_element_type=jnp.float32) * 0.125
    )
    return (grad_query, grad_keys, grad_values)


def body(
    hidden_in,
    lengths,
    ln1_gain,
    ln1_shift,
    w_qkv,
    bias_q,
    bias_v,
    w_out,
    bias_out,
    ln2_gain,
    ln2_shift,
    w_up,
    bias_up,
    w_down,
    bias_down,
    cotangent,
):
    tokens_in = jnp.transpose(hidden_in)
    grad_given = jnp.transpose(cotangent)
    rows = tokens_in.shape[0]
    slots = lengths.shape[0]
    span = rows // slots
    heads_here = w_qkv.shape[1] // (3 * HEAD)
    head_ids = lax.axis_index("col") * heads_here + jnp.arange(heads_here)
    slopes = jnp.exp2(-8.0 * (head_ids.astype(jnp.float32) + 1.0) / HEADS)
    qkv_full, up_full, out_full, down_full = (
        lax.all_gather(w_qkv, "row", axis=0, tiled=True),
        lax.all_gather(w_up, "row", axis=0, tiled=True),
        lax.all_gather(w_out, "row", axis=1, tiled=True),
        lax.all_gather(w_down, "row", axis=1, tiled=True),
    )
    normed1, inverse1, low1 = norm_forward(tokens_in, ln1_gain, ln1_shift)
    rows1 = gather_rows(low1)
    mixed = jnp.dot(rows1, qkv_full, preferred_element_type=jnp.float32).reshape(
        rows, heads_here, 3, HEAD
    )
    query = (
        (mixed[:, :, 0] + bias_q.reshape(heads_here, HEAD))
        .astype(jnp.bfloat16)
        .reshape(slots, span, heads_here, HEAD)
    )
    keys = mixed[:, :, 1].astype(jnp.bfloat16).reshape(slots, span, heads_here, HEAD)
    values = (
        (mixed[:, :, 2] + bias_v.reshape(heads_here, HEAD))
        .astype(jnp.bfloat16)
        .reshape(slots, span, heads_here, HEAD)
    )
    attended, lse = lax.map(partial(forward_slot, slopes), (query, keys, values, lengths))
    attn_low = attended.reshape(rows, heads_here * HEAD).astype(jnp.bfloat16)
    projected = lax.psum_scatter(
        jnp.dot(attn_low, out_full, preferred_element_type=jnp.float32),
        "col",
        scatter_dimension=1,
        tiled=True,
    )
    hidden1 = tokens_in + projected + bias_out
    normed2, inverse2, low2 = norm_forward(hidden1, ln2_gain, ln2_shift)
    rows2 = gather_rows(low2)
    pre = jnp.dot(rows2, up_full, preferred_element_type=jnp.float32) + bias_up
    act, act_pull = jax.vjp(partial(jax.nn.gelu, approximate=True), pre)
    act_low = act.astype(jnp.bfloat16)
    down_terms = jnp.dot(act_low, down_full, preferred_element_type=jnp.float32)
    result = (
        hidden1
        + lax.psum_scatter(
            down_terms.astype(jnp.bfloat16), "col", scatter_dimension=1, tiled=True
        ).astype(jnp.float32)
        + bias_down
    )
    grad_low = grad_given.astype(jnp.bfloat16)
    grad_full = lax.all_gather(grad_low, "col", axis=1, tiled=True)
    grad_down = jnp.einsum("tf,td->fd", act_low, grad_full, preferred_element_type=jnp.float32)
    grad_act = jnp.einsum("td,fd->tf", grad_full, down_full, preferred_element_type=jnp.float32)
    grad_pre = act_pull(grad_act)[0]
    grad_pre_low = grad_pre.astype(jnp.bfloat16)
    grad_up = jnp.einsum("td,tf->df", rows2, grad_pre_low, preferred_element_type=jnp.float32)
    grad_norm2 = back_columns(
        jnp.einsum("tf,df->td", grad_pre_low, up_full, preferred_element_type=jnp.float32)
    )
    grad_hidden1 = grad_given + norm_backward(grad_norm2, normed2, inverse2, ln2_gain)
    branch_low = grad_hidden1.astype(jnp.bfloat16)
    grad_branch = lax.all_gather(branch_low, "col", axis=1, tiled=True)
    grad_outw = jnp.einsum("tc,td->cd", attn_low, grad_branch, preferred_element_type=jnp.float32)
    grad_attn = jnp.einsum(
        "td,cd->tc", grad_branch, out_full, preferred_element_type=jnp.float32
    ).astype(jnp.bfloat16)
    grad_attn = grad_attn.reshape(slots, span, heads_here, HEAD)
    grad_query, grad_keys, grad_values = lax.map(
        partial(backward_slot, slopes), (query, keys, values, grad_attn, lse, lengths)
    )
    stacked = jnp.stack((grad_query, grad_keys, grad_values), axis=3).reshape(
        rows, 3 * heads_here * HEAD
    )
    stacked_low = stacked.astype(jnp.bfloat16)
    grad_qkv = jnp.einsum("td,tc->dc", rows1, stacked_low, preferred_element_type=jnp.float32)
    grad_norm1 = back_columns(
        jnp.einsum("tc,dc->td", stacked_low, qkv_full, preferred_element_type=jnp.float32)
    )
    grad_input = grad_hidden1 + norm_backward(grad_norm1, normed1, inverse1, ln1_gain)
    small = lax.psum(
        (
            jnp.sum(grad_norm1 * normed1, axis=0),
            jnp.sum(grad_norm1, axis=0),
            jnp.sum(grad_query.reshape(rows, heads_here * HEAD), axis=0),
            jnp.sum(grad_values.reshape(rows, heads_here * HEAD), axis=0),
            jnp.sum(grad_hidden1, axis=0),
            jnp.sum(grad_norm2 * normed2, axis=0),
            jnp.sum(grad_norm2, axis=0),
            jnp.sum(grad_pre, axis=0),
            jnp.sum(grad_given, axis=0),
        ),
        ("dp", "row"),
    )
    local = (grad_qkv, grad_up, grad_outw, grad_down)
    whole = (
        lax.psum(local[0].astype(jnp.bfloat16), "dp").astype(jnp.float32),
        lax.psum(local[1].astype(jnp.bfloat16), "dp").astype(jnp.float32),
        lax.psum(local[2].astype(jnp.bfloat16), "dp").astype(jnp.float32),
        lax.psum(local[3].astype(jnp.bfloat16), "dp").astype(jnp.float32),
    )
    summed = (
        lax.psum_scatter(
            whole[0].astype(jnp.bfloat16), "row", scatter_dimension=0, tiled=True
        ).astype(jnp.float32),
        lax.psum_scatter(
            whole[1].astype(jnp.bfloat16), "row", scatter_dimension=0, tiled=True
        ).astype(jnp.float32),
        lax.psum_scatter(
            whole[2].astype(jnp.bfloat16), "row", scatter_dimension=1, tiled=True
        ).astype(jnp.float32),
        lax.psum_scatter(
            whole[3].astype(jnp.bfloat16), "row", scatter_dimension=1, tiled=True
        ).astype(jnp.float32),
    )
    return (
        jnp.transpose(result),
        jnp.transpose(grad_input),
        small[0],
        small[1],
        summed[0],
        small[2],
        small[3],
        summed[2],
        small[4],
        small[5],
        small[6],
        summed[1],
        small[7],
        summed[3],
        small[8],
    )


def solution(mesh):
    return jax.shard_map(
        body,
        mesh=mesh,
        in_specs=(
            P("col", ("dp", "row")),
            P(("dp", "row")),
            P("col"),
            P("col"),
            P("row", "col"),
            P("col"),
            P("col"),
            P("col", "row"),
            P("col"),
            P("col"),
            P("col"),
            P("row", "col"),
            P("col"),
            P("col", "row"),
            P("col"),
            P("col", ("dp", "row")),
        ),
        out_specs=(
            P("col", ("dp", "row")),
            P("col", ("dp", "row")),
            P("col"),
            P("col"),
            P("row", "col"),
            P("col"),
            P("col"),
            P("col", "row"),
            P("col"),
            P("col"),
            P("col"),
            P("row", "col"),
            P("col"),
            P("col", "row"),
            P("col"),
        ),
        check_vma=False,
    )
```

profile of v0, /device:TPU:0, one launch (start us, length us, event | category | flops | bytes accessed | tf_op | source)
XLA Modules:
  0.0 1329.2 jit_solution(10266186835196599832)
XLA Ops:
  17.6 9.6 all-reduce.4
  34.8 53.8 %all-gather.9.cloned.1.call-done = bf16[2048,1024]{1,0:T(8,128)(2,1)} async-done(((bf16[2048,512]{1,0:T(8,128)(2,1)}), bf16[2048,1024]{1,0:T(8,128)(2,1)}) %all-gather.9.cloned.1.call-update) | async-done | bytes 4194320 | tf_op jit(solution)/shard_map/all_gather | solution.py:31
  88.6 65.1 %all-gather.11.cloned.1.call-done = bf16[1024,1536]{1,0:T(8,128)(2,1)} async-done(((bf16[256,1536]{1,0:T(8,128)(2,1)}), bf16[1024,1536]{1,0:T(8,128)(2,1)}) %all-gather.11.cloned.1.call-update) | async-done | bytes 3145744 | tf_op jit(solution)/shard_map/all_gather | solution.py:109
  153.7 9.8 fusion.100
  198.4 53.5 %while.30 = (s32[]{:T(128)}, bf16[4,512,8,64]{1,3,2,0:T(8,128)(2,1)}, f32[4,8,512]{2,1,0:T(8,128)}, bf16[4,512,8,64]{1,3,2,0:T(8,128)(2,1)}, s32[4]{0:T(128)S(1)...) while((s32[]{:T(128)}, ...), condition=%wide.region_7.8_spmd.clone.clone, body=%wide.region_4.7_spmd.clone.sunk.clone | while | flops 575664640 | bytes 49942764 | solution.py:130
  266.0 97.4 %reduce-scatter.9.cloned.1.call-done = f32[2048,512]{1,0:T(8,128)} async-done(((f32[2048,1024]{1,0:T(8,128)}), f32[2048,512]{1,0:T(8,128)}) %reduce-scatter.9.cloned.1.call-update) | async-done | bytes 4194320 | tf_op jit(solution)/shard_map/reduce_scatter | solution.py:132
  390.2 55.4 %all-gather.17.cloned.1.call-done = bf16[1024,2048]{1,0:T(8,128)(2,1)} async-done(((bf16[256,2048]{1,0:T(8,128)(2,1)}), bf16[1024,2048]{1,0:T(8,128)(2,1)}) %all-gather.17.cloned.1.call-update) | async-done | bytes 4194320 | tf_op jit(solution)/shard_map/all_gather | solution.py:110
  445.6 56.8 %all-gather.15.cloned.1.call-done = bf16[2048,1024]{1,0:T(8,128)(2,1)} async-done(((bf16[2048,512]{1,0:T(8,128)(2,1)}), bf16[2048,1024]{1,0:T(8,128)(2,1)}) %all-gather.15.cloned.1.call-update) | async-done | bytes 4194320 | tf_op jit(solution)/shard_map/all_gather | solution.py:31
  502.4 15.3 %fusion.102 = f32[2048,2048]{1,0:T(8,128)} fusion(bf16[2048,1024]{1,0:T(8,128)(2,1)} %all-gather.15.cloned.1.call-done, bf16[1024,2048]{1,0:T(8,128)(2,1)} %all-gather.17.cloned.1.call-done), kind=kOutput, calls=%fused_computation.144 | convolution fusion | flops 8589934592 | bytes 25165824 | tf_op jit(solution)/shard_map/dot_general | solution.py:141
  517.7 43.1 %all-gather.21.cloned.1.call-done = bf16[2048,1024]{1,0:T(8,128)(2,1)} async-done(((bf16[2048,512]{1,0:T(8,128)(2,1)}), bf16[2048,1024]{1,0:T(8,128)(2,1)}) %all-gather.21.cloned.1.call-update) | async-done | bytes 4194320 | tf_op jit(solution)/shard_map/all_gather | solution.py:153
  560.8 82.2 %all-gather.19.cloned.1.call-done = bf16[2048,1024]{1,0:T(8,128)(2,1)} async-done(((bf16[2048,256]{1,0:T(8,128)(2,1)}), bf16[2048,1024]{1,0:T(8,128)(2,1)}) %all-gather.19.cloned.1.call-update) | async-done | bytes 4194320 | tf_op jit(solution)/shard_map/all_gather | solution.py:112
  643.0 27.5 %fusion.91 = (f32[2048]{0:T(1024)}, bf16[2048,2048]{1,0:T(8,128)(2,1)}, bf16[2048,2048]{1,0:T(8,128)(2,1)}) fusion(f32[2048,2048]{1,0:T(8,128)} %fusion.102, f32[2048]{0:T(1024)S(1)} %copy-done.34, bf16[2048,1024]{1,0:T(8,128)(2,1)} %all-gather.21.cloned.1.call-done, bf16[2048,1024]{1,0:T(8,128)(2,1)} %all-gather.19.cloned.1.call-done), kind=kOutput, calls=%fused_computation.136 | convolution fusion | flops 8690595840 | bytes 41959424 | tf_op jit(solution)/shard_map/td,fd->tf/dot_general | solution.py:155
  670.5 13.0 fusion.84
  683.6 13.8 %convolution_convert_fusion.2 = bf16[2048,1024]{1,0:T(8,128)(2,1)} fusion(bf16[2048,2048]{1,0:T(8,128)(2,1)} %get-tuple-element.304, bf16[2048,1024]{1,0:T(8,128)(2,1)} %all-gather.19.cloned.1.call-done), kind=kOutput, calls=%fused_computation.122 | convolution fusion | flops 8592031744 | bytes 16777216 | tf_op jit(solution)/shard_map/dot_general | solution.py:144
  697.4 38.7 %reduce-scatter.13.cloned.1.call-done = bf16[2048,512]{1,0:T(8,128)(2,1)} async-done(((bf16[2048,1024]{1,0:T(8,128)(2,1)}), bf16[2048,512]{1,0:T(8,128)(2,1)}) %reduce-scatter.13.cloned.1.call-update) | async-done | bytes 2097168 | tf_op jit(solution)/shard_map/reduce_scatter | solution.py:35
  747.9 44.8 %reduce-scatter.11.cloned.1.call-done = bf16[2048,512]{1,0:T(8,128)(2,1)} async-done(((bf16[2048,1024]{1,0:T(8,128)(2,1)}), bf16[2048,512]{1,0:T(8,128)(2,1)}) %reduce-scatter.11.cloned.1.call-update) | async-done | bytes 2097168 | tf_op jit(solution)/shard_map/reduce_scatter | solution.py:147
  792.8 8.2 fusion.93
  804.6 14.2 %convolution_convert_fusion.3 = bf16[2048,1024]{1,0:T(8,128)(2,1)} fusion(bf16[2048,2048]{1,0:T(8,128)(2,1)} %get-tuple-element.304, bf16[2048,1024]{1,0:T(8,128)(2,1)} %all-gather.21.cloned.1.call-done), kind=kOutput, calls=%fused_computation.123 | convolution fusion | flops 8592031744 | bytes 16777216 | tf_op jit(solution)/shard_map/tf,td->fd/dot_general | solution.py:154
  818.8 14.1 %fusion.87 = bf16[1024,2048]{1,0:T(8,128)(2,1)} fusion(bf16[2048,1024]{1,0:T(8,128)(2,1)} %all-gather.15.cloned.1.call-done, bf16[2048,2048]{1,0:T(8,128)(2,1)} %get-tuple-element.296), kind=kOutput, calls=%fused_computation.121 | convolution fusion | flops 8592031744 | bytes 16777216 | tf_op jit(solution)/shard_map/td,tf->df/dot_general | solution.py:158
  833.0 28.5 %all-gather.23.cloned.1.call-done = bf16[2048,1024]{1,0:T(8,128)(2,1)} async-done(((bf16[2048,512]{1,0:T(8,128)(2,1)}), bf16[2048,1024]{1,0:T(8,128)(2,1)}) %all-gather.23.cloned.1.call-update) | async-done | bytes 4194320 | tf_op jit(solution)/shard_map/all_gather | solution.py:164
  880.7 133.4 %while.31 = (s32[]{:T(128)}, f32[4,512,8,64]{1,3,2,0:T(8,128)}, bf16[4,512,8,64]{1,3,2,0:T(8,128)(2,1)}, f32[4,512,8,64]{1,3,2,0:T(8,128)}, bf16[4,512,8,64]{1,3...) while((s32[]{:T(128)}, f32[4,512,8,64]{1,3,2,0:T(8,128)}, ...), condition=%wide.region_21.22_spmd.clone.clone, body=%wide.region_19.21_spmd.clone.sunk.clone | while | flops 1366815232 | bytes 122771752 | solution.py:170
  885.3 8.9 multiply_reduce_fusion.4
  918.7 8.9 multiply_reduce_fusion.4
  952.0 8.9 multiply_reduce_fusion.4
  985.3 8.9 multiply_reduce_fusion.4
  1022.4 8.3 copy.58
  1039.0 8.4 convolution_convert_fusion
  1050.7 61.7 %reduce-scatter.17.cloned.1.call-done = bf16[256,1536]{1,0:T(8,128)(2,1)} async-done(((bf16[1024,1536]{1,0:T(8,128)(2,1)}), bf16[256,1536]{1,0:T(8,128)(2,1)}) %reduce-scatter.17.cloned.1.call-update) | async-done | bytes 786448 | tf_op jit(solution)/shard_map/reduce_scatter | solution.py:204
  1112.4 11.7 convolution_convert_fusion.1
  1132.2 51.7 %all-reduce.8.cloned.1.call-done = (bf16[256,1536]{1,0:T(8,128)(2,1)}, bf16[512,256]{1,0:T(8,128)(2,1)}, bf16[256,2048]{1,0:T(8,128)(2,1)}, bf16[2048,256]{1,0:T(8,128)(2,1)}) async-done(((bf16[256,1536]{1,0:T(8,128)(2,1)}, bf16[512,256]{1,0:T(8,128)(2,1)}, bf16[256,2048]{1,0:T(8,128)(2,1)}, bf16[2048,256]{1,0:T(8,128)(2,1)}), (bf16[256,1536]{1,0:T(8,128)(2,1)}, bf16[512,256]{1,0:T(8,128)(2,1)}, ...) | async-done | bytes 3145744 | tf_op jit(solution)/shard_map/psum | solution.py:198
  1192.5 47.9 %reduce-scatter.15.cloned.1.call-done = bf16[2048,512]{1,0:T(8,128)(2,1)} async-done(((bf16[2048,1024]{1,0:T(8,128)(2,1)}), bf16[2048,512]{1,0:T(8,128)(2,1)}) %reduce-scatter.15.cloned.1.call-update) | async-done | bytes 2097168 | tf_op jit(solution)/shard_map/reduce_scatter | solution.py:35
  1262.6 59.9 %all-reduce = (f32[512]{0:T(512)}, f32[512]{0:T(512)}, f32[512]{0:T(512)}, f32[512]{0:T(512)}, f32[512]{0:T(512)}, /*index=5*/f32[512]{0:T(512)}, f32[512]{0:T(512)}, f32[2048]{0:T(1024)}, f32[512]{0:T(512)}) all-reduce(f32[512]{0:T(512)S(1)} %get-tuple-element.228, ...), channel_id=1, replica_groups=mesh['dp'=4,'row'=4,'col'=2] {'dp','row'}, use_global_device_ids=true, to_apply=%region_28.29 | all-reduce | flops 6144 | bytes 49152 | tf_op jit(solution)/shard_map/psum | solution.py:182
  (278 shorter events, 337.5 us)
Async XLA Ops:
  7.2 81.4 %all-gather.9.cloned.1.call-start = ((), (), s32[]{:S(2)}) async-start(), calls=%async_computation.8 | async-start | bytes 6291456 | tf_op jit(solution)/shard_map/all_gather | solution.py:31
  12.6 15.2 %copy-start.19 = (f32[512]{0:T(512)S(1)}, f32[512]{0:T(512)}, u32[]{:S(2)}) copy-start(f32[512]{0:T(512)} %param.22) | copy-start | bytes 6148
  12.6 15.2 %copy-start.25 = (f32[512]{0:T(512)S(1)}, f32[512]{0:T(512)}, u32[]{:S(2)}) copy-start(f32[512]{0:T(512)} %param.23) | copy-start | bytes 6148
  31.4 122.2 %all-gather.11.cloned.1.call-start = ((), (), s32[]{:S(2)}) async-start(), calls=%async_computation.9 | async-start | bytes 3932160 | tf_op jit(solution)/shard_map/all_gather | solution.py:109
  32.2 225.6 %all-gather.13.cloned.1.call-start = ((), (), s32[]{:S(2)}) async-start(), calls=%async_computation.10 | async-start | bytes 1310720 | tf_op jit(solution)/shard_map/all_gather | solution.py:111
  32.9 330.4 %reduce-scatter.9.cloned.1.call-start = ((), (), s32[]{:S(2)}) async-start(), calls=%async_computation.11 | async-start | bytes 12582912 | tf_op jit(solution)/shard_map/reduce_scatter | solution.py:132
  33.2 130.3 %copy-start.3 = (bf16[4,512,8,64]{1,3,2,0:T(8,128)(2,1)}, bf16[4,512,8,64]{1,3,2,0:T(8,128)(2,1)S(1)}, u32[]{:S(2)}) copy-start(bf16[4,512,8,64]{1,3,2,0:T(8,128)(2,1)S(1)} %fusion.99) | copy-start | bytes 6291460
  265.3 98.1 %copy-start.30 = (f32[512]{0:T(512)S(1)}, f32[512]{0:T(512)}, u32[]{:S(2)}) copy-start(f32[512]{0:T(512)} %param.28) | copy-start | bytes 6148
  265.3 180.3 %all-gather.17.cloned.1.call-start = ((), (), s32[]{:S(2)}) async-start(), calls=%async_computation.13 | async-start | bytes 5242880 | tf_op jit(solution)/shard_map/all_gather | solution.py:110
  265.9 110.3 %copy-start.18 = (f32[512]{0:T(512)S(1)}, f32[512]{0:T(512)}, u32[]{:S(2)}) copy-start(f32[512]{0:T(512)} %param.29) | copy-start | bytes 6148
  265.9 110.3 %copy-start.26 = (f32[512]{0:T(512)S(1)}, f32[512]{0:T(512)}, u32[]{:S(2)}) copy-start(f32[512]{0:T(512)} %param.30) | copy-start | bytes 6148
  265.9 236.5 %all-gather.15.cloned.1.call-start = ((), (), s32[]{:S(2)}) async-start(), calls=%async_computation.12 | async-start | bytes 6291456 | tf_op jit(solution)/shard_map/all_gather | solution.py:31
  379.9 180.9 %all-gather.21.cloned.1.call-start = ((), (), s32[]{:S(2)}) async-start(), calls=%async_computation.16 | async-start | bytes 6291456 | tf_op jit(solution)/shard_map/all_gather | solution.py:153
  389.4 253.6 %all-gather.19.cloned.1.call-start = ((), (), s32[]{:S(2)}) async-start(), calls=%async_computation.14 | async-start | bytes 5242880 | tf_op jit(solution)/shard_map/all_gather | solution.py:112
  390.2 252.9 %copy-start.34 = (f32[2048]{0:T(1024)S(1)}, f32[2048]{0:T(1024)}, u32[]{:S(2)}) copy-start(f32[2048]{0:T(1024)} %param.32) | copy-start | bytes 24580
  390.2 346.0 %reduce-scatter.13.cloned.1.call-start = ((), (), s32[]{:S(2)}) async-start(), calls=%async_computation.17 | async-start | bytes 6291456 | tf_op jit(solution)/shard_map/reduce_scatter | solution.py:35
  643.0 27.5 %copy-start.32 = (bf16[1024,2048]{1,0:T(8,128)(2,1)S(1)}, bf16[1024,2048]{1,0:T(8,128)(2,1)}, u32[]{:S(2)}) copy-start(bf16[1024,2048]{1,0:T(8,128)(2,1)} %all-gather.17.cloned.1.call-done) | copy-start | bytes 12582916
  683.5 109.2 %reduce-scatter.11.cloned.1.call-start = ((), (), s32[]{:S(2)}) async-start(), calls=%async_computation.15 | async-start | bytes 6291456 | tf_op jit(solution)/shard_map/reduce_scatter | solution.py:147
  697.4 95.4 %copy-start.27 = (f32[512]{0:T(512)S(1)}, f32[512]{0:T(512)}, u32[]{:S(2)}) copy-start(f32[512]{0:T(512)} %param.34) | copy-start | bytes 6148
  697.4 164.1 %all-gather.23.cloned.1.call-start = ((), (), s32[]{:S(2)}) async-start(), calls=%async_computation.18 | async-start | bytes 6291456 | tf_op jit(solution)/shard_map/all_gather | solution.py:164
  736.2 56.6 %copy-start.7 = (bf16[2048,512]{1,0:T(8,128)(2,1)S(1)}, bf16[2048,512]{1,0:T(8,128)(2,1)}, u32[]{:S(2)}) copy-start(bf16[2048,512]{1,0:T(8,128)(2,1)} %reduce-scatter.13.cloned.1.call-done) | copy-start | bytes 6291460
  804.5 242.9 %reduce-scatter.23.cloned.1.call-start = ((), (), s32[]{:S(2)}) async-start(), calls=%async_computation.23 | async-start | bytes 5242880 | tf_op jit(solution)/shard_map/reduce_scatter | solution.py:213
  818.8 228.7 %reduce-scatter.21.cloned.1.call-start = ((), (), s32[]{:S(2)}) async-start(), calls=%async_computation.22 | async-start | bytes 5242880 | tf_op jit(solution)/shard_map/reduce_scatter | solution.py:207
  832.9 28.6 %copy-start.33 = (bf16[512,1024]{1,0:T(8,128)(2,1)S(1)}, bf16[512,1024]{1,0:T(8,128)(2,1)}, u32[]{:S(2)}) copy-start(bf16[512,1024]{1,0:T(8,128)(2,1)} %all-gather.13.cloned.1.call-done) | copy-start | bytes 3145732
  832.9 217.7 %reduce-scatter.19.cloned.1.call-start = ((), (), s32[]{:S(2)}) async-start(), calls=%async_computation.21 | async-start | bytes 1310720 | tf_op jit(solution)/shard_map/reduce_scatter | solution.py:210
  1014.1 98.2 %reduce-scatter.17.cloned.1.call-start = ((), (), s32[]{:S(2)}) async-start(), calls=%async_computation.20 | async-start | bytes 3932160 | tf_op jit(solution)/shard_map/reduce_scatter | solution.py:204
  1047.4 136.4 %all-reduce.8.cloned.1.call-start = ((), (), s32[]{:S(2)}) async-start(), calls=%async_computation.24 | async-start | bytes 6291456 | tf_op jit(solution)/shard_map/psum | solution.py:198
  1112.4 128.0 %reduce-scatter.15.cloned.1.call-start = ((), (), s32[]{:S(2)}) async-start(), calls=%async_computation.19 | async-start | bytes 6291456 | tf_op jit(solution)/shard_map/reduce_scatter | solution.py:35
  1185.7 54.7 %copy-start.15 = (f32[2048]{0:T(1024)S(1)}, f32[2048]{0:T(1024)}, u32[]{:S(2)}) copy-start(f32[2048]{0:T(1024)} %copy-done.14) | copy-start | bytes 24580
  1185.7 54.7 %copy-start.17 = (f32[2048]{0:T(1024)S(1)}, f32[2048]{0:T(1024)}, u32[]{:S(2)}) copy-start(f32[2048]{0:T(1024)} %copy-done.16) | copy-start | bytes 24580
  1185.7 54.7 %copy-start.20 = (f32[512]{0:T(512)S(1)}, f32[512]{0:T(512)}, u32[]{:S(2)}) copy-start(f32[512]{0:T(512)} %param.22) | copy-start | bytes 6148
  1240.4 11.2 copy-start.8
  (37 other events, 166.0 us)
Sparse Core Ops, SparseCore 0:
  31.5 56.9 all-gather.8
  90.1 63.4 all-gather.10
  155.2 28.8 all-gather.12
  265.4 97.8 reduce-scatter.8
  364.8 80.7 all-gather.16
  447.1 55.2 all-gather.14
  504.0 56.7 all-gather.20
  562.4 80.5 all-gather.18
  683.6 52.4 reduce-scatter.12
  738.3 54.3 reduce-scatter.10
  804.7 56.8 all-gather.22
  863.8 76.7 reduce-scatter.22
  942.8 77.3 reduce-scatter.20
  1023.0 27.6 reduce-scatter.18
  1053.4 58.8 reduce-scatter.16
  1114.8 68.9 all-reduce.7
  1186.0 54.3 reduce-scatter.14
where the time goes:
time: 1340 us; the launch traced here: 1330 us
  waiting for transfers between devices  733 us (55%)
  matrix products  269 us (20%)
  other arithmetic  124 us (9%)
  local copies, waits for them, and re-layouts  96.6 us (7%)
  blocking collectives  90.2 us (7%)
  between operations  14.5 us (1%)
    all_gather x2, waiting for transfers between devices, gather_rows(): return lax.all_gather(value, 'col', axis=1, tiled=True)  111 us
    reduce_scatter x1, waiting for transfers between devices, body(): lax.psum_scatter(jnp.dot(attn_low, out_full, preferred_element_type=jnp.f...  97.4 us
    reduce_scatter x2, waiting for transfers between devices, back_columns(): lax.psum_scatter(value.astype(jnp.bfloat16), 'col', scatter_dimension=1,...  86.7 us
    all_gather x1, waiting for transfers between devices, body(): lax.all_gather(w_down, 'row', axis=1, tiled=True)  82.2 us
    all_gather x1, waiting for transfers between devices, body(): lax.all_gather(w_qkv, 'row', axis=0, tiled=True)  65.1 us
    reduce_scatter x1, waiting for transfers between devices, body(): lax.psum_scatter(whole[0].astype(jnp.bfloat16), 'row', scatter_dimension=...  61.7 us
    psum x1, blocking collectives, body(): lax.psum((jnp.sum(grad_norm1 * normed1, axis=0), jnp.sum(grad_norm1, axis...  59.9 us
    all_gather x1, waiting for transfers between devices, body(): lax.all_gather(w_up, 'row', axis=0, tiled=True)  55.4 us
  transfers between devices with their start and end apart: 17, of which 14 were waited for; matrix products, arithmetic and copies ran while one was open for 30% of the time, Pallas kernels for 0%

commit v1 on v0

--- a/solution.py
+++ b/solution.py
@@ -8,6 +8,28 @@
 HEAD = 64
 EPS = 1e-05
 NEG = -1e30
+
+
+def joined_along(tiles, dim):
+    tiles = jnp.moveaxis(tiles, 0, dim)
+    shape = tiles.shape
+    return tiles.reshape(*shape[:dim], shape[dim] * shape[dim + 1], *shape[dim + 2 :])
+
+
+def collect(x, axis, dim):
+    size = lax.axis_size(axis)
+    pairs = [(i, (i + 1) % size) for i in range(size)]
+    back = [(b, a) for a, b in pairs]
+    lower, upper = ([], [])
+    for step in range(size - 1):
+        if step % 2 == 0:
+            lower.append(lax.ppermute(lower[-1] if lower else x, axis, pairs))
+        else:
+            upper.append(lax.ppermute(upper[-1] if upper else x, axis, back))
+    pieces = jnp.stack([*lower[::-1], x, *upper])
+    shift = lax.axis_index(axis) - len(lower)
+    pieces = pieces[(jnp.arange(size) - shift) % size]
+    return joined_along(pieces, dim)
 
 
 def norm_forward(value, gain, shift):
@@ -107,7 +129,7 @@
     slopes = jnp.exp2(-8.0 * (head_ids.astype(jnp.float32) + 1.0) / HEADS)
     qkv_full, up_full, out_full, down_full = (
         lax.all_gather(w_qkv, "row", axis=0, tiled=True),
-        lax.all_gather(w_up, "row", axis=0, tiled=True),
+        collect(w_up, "row", 0),
         lax.all_gather(w_out, "row", axis=1, tiled=True),
         lax.all_gather(w_down, "row", axis=1, tiled=True),
     )

time: 1340 us -> 1260 us (0.940)
  waiting for transfers between devices: 733 us -> 650 us
    all_gather x1 -> x0, waiting for transfers between devices: 55.4 us -> none  [body(): lax.all_gather(w_up, 'row', axis=0, tiled=True)]
    ppermute x0 -> x3, waiting for transfers between devices: none -> 44 us  [the longest x1 23.6 us: collect(): upper.append(lax.ppermute(upper[-1] if upper else x, axis, back))]
    all_gather x1, waiting for transfers between devices: 43.1 us -> 0.01 us  [body(): grad_full = lax.all_gather(grad_low, 'col', axis=1, tiled=True)]
    all_gather x2, waiting for transfers between devices: 111 us -> 95.1 us  [gather_rows(): return lax.all_gather(value, 'col', axis=1, tiled=True)]
    all_gather x1, waiting for transfers between devices: 82.2 us -> 67.7 us  [body(): lax.all_gather(w_down, 'row', axis=1, tiled=True)]
    dot_general x4, matrix products: 23.9 us -> 9.69 us  [backward_slot(): jnp.einsum('hqk,qhd->khd', probs.astype(jnp.bfloat16), grad_out, preferre...]
    unnamed x76 -> x82, local copies, waits for them, and re-layouts: 47.8 us -> 51.1 us
  transfers between devices with their start and end apart: 17 -> 19, of which waited for: 14 -> 14; matrix products, arithmetic and copies ran while one was open for 30% -> 31% of each run, Pallas kernels for 0% -> 0%
where the time goes in v1:
time: 1260 us; the launch traced here: 1250 us
  waiting for transfers between devices  650 us (52%)
  matrix products  256 us (20%)
  other arithmetic  126 us (10%)
  local copies, waits for them, and re-layouts  108 us (9%)
  blocking collectives  90.4 us (7%)
  between operations  14.5 us (1%)
    all_gather x2, waiting for transfers between devices, gather_rows(): return lax.all_gather(value, 'col', axis=1, tiled=True)  95.1 us
    reduce_scatter x2, waiting for transfers between devices, back_columns(): lax.psum_scatter(value.astype(jnp.bfloat16), 'col', scatter_dimension=1,...  89.4 us
    reduce_scatter x1, waiting for transfers between devices, body(): lax.psum_scatter(jnp.dot(attn_low, out_full, preferred_element_type=jnp.f...  87.9 us
    all_gather x1, waiting for transfers between devices, body(): lax.all_gather(w_down, 'row', axis=1, tiled=True)  67.7 us
    all_gather x1, waiting for transfers between devices, body(): lax.all_gather(w_qkv, 'row', axis=0, tiled=True)  65.1 us
    reduce_scatter x1, waiting for transfers between devices, body(): lax.psum_scatter(whole[0].astype(jnp.bfloat16), 'row', scatter_dimension=...  61.7 us
    psum x1, blocking collectives, body(): lax.psum((jnp.sum(grad_norm1 * normed1, axis=0), jnp.sum(grad_norm1, axis...  59.9 us
    psum x1, waiting for transfers between devices, body(): lax.psum(local[0].astype(jnp.bfloat16), 'dp').astype(jnp.float32)  51.7 us
  transfers between devices with their start and end apart: 19, of which 14 were waited for; matrix products, arithmetic and copies ran while one was open for 31% of the time, Pallas kernels for 0%

profile of v1, /device:TPU:0, one launch (start us, length us, event | category | flops | bytes accessed | tf_op | source)
XLA Modules:
  0.0 1250.9 jit_solution(3859143876658172658)
XLA Ops:
  17.6 9.6 all-reduce.4
  34.8 53.8 %all-gather.8.cloned.1.call-done = bf16[2048,1024]{1,0:T(8,128)(2,1)} async-done(((bf16[2048,512]{1,0:T(8,128)(2,1)}), bf16[2048,1024]{1,0:T(8,128)(2,1)}) %all-gather.8.cloned.1.call-update) | async-done | bytes 4194320 | tf_op jit(solution)/shard_map/all_gather | solution.py:53
  88.6 65.1 %all-gather.10.cloned.1.call-done = bf16[1024,1536]{1,0:T(8,128)(2,1)} async-done(((bf16[256,1536]{1,0:T(8,128)(2,1)}), bf16[1024,1536]{1,0:T(8,128)(2,1)}) %all-gather.10.cloned.1.call-update) | async-done | bytes 3145744 | tf_op jit(solution)/shard_map/all_gather | solution.py:131
  153.7 9.8 fusion.102
  198.4 53.3 %while.30 = (s32[]{:T(128)}, bf16[4,512,8,64]{1,3,2,0:T(8,128)(2,1)}, f32[4,8,512]{2,1,0:T(8,128)}, bf16[4,512,8,64]{1,3,2,0:T(8,128)(2,1)}, s32[4]{0:T(128)S(1)...) while((s32[]{:T(128)}, ...), condition=%wide.region_7.8_spmd.clone.clone, body=%wide.region_4.7_spmd.clone.sunk.clone | while | flops 575664640 | bytes 33165512 | solution.py:152
  275.2 87.9 %reduce-scatter.9.cloned.1.call-done = f32[2048,512]{1,0:T(8,128)} async-done(((f32[2048,1024]{1,0:T(8,128)}), f32[2048,512]{1,0:T(8,128)}) %reduce-scatter.9.cloned.1.call-update) | async-done | bytes 4194320 | tf_op jit(solution)/shard_map/reduce_scatter | solution.py:154
  383.9 23.6 %collective-permute-done.2 = bf16[256,2048]{1,0:T(8,128)(2,1)S(1)} collective-permute-done((bf16[256,2048]{1,0:T(8,128)(2,1)S(1)}, bf16[256,2048]{1,0:T(8,128)(2,1)S(1)}, u32[]{:S(2)}, u32[]{:S(2)}) %collective-permute-start.2) | collective-permute-done | bytes 1048608 | tf_op jit(solution)/shard_map/ppermute | solution.py:28
  407.5 20.4 %collective-permute-done.1 = bf16[256,2048]{1,0:T(8,128)(2,1)} collective-permute-done((bf16[256,2048]{1,0:T(8,128)(2,1)S(1)}, bf16[256,2048]{1,0:T(8,128)(2,1)}, u32[]{:S(2)}, u32[]{:S(2)}) %collective-permute-start.1) | collective-permute-done | bytes 1048608 | tf_op jit(solution)/shard_map/ppermute | solution.py:26
  436.4 67.7 %all-gather.16.cloned.1.call-done = bf16[2048,1024]{1,0:T(8,128)(2,1)} async-done(((bf16[2048,256]{1,0:T(8,128)(2,1)}), bf16[2048,1024]{1,0:T(8,128)(2,1)}) %all-gather.16.cloned.1.call-update) | async-done | bytes 4194320 | tf_op jit(solution)/shard_map/all_gather | solution.py:134
  504.1 15.3 %fusion.104 = f32[2048,2048]{1,0:T(8,128)} fusion(bf16[2048,1024]{1,0:T(8,128)(2,1)} %all-gather.18.cloned.1.call-done, bf16[2048,1024]{1,0:T(8,128)(2,1)} %all-gather.16.cloned.1.call-done), kind=kOutput, calls=%fused_computation.153 | convolution fusion | flops 8589934592 | bytes 25165824 | tf_op jit(solution)/shard_map/td,fd->tf/dot_general | solution.py:177
  519.4 41.3 %all-gather.14.cloned.1.call-done = bf16[2048,1024]{1,0:T(8,128)(2,1)} async-done(((bf16[2048,512]{1,0:T(8,128)(2,1)}), bf16[2048,1024]{1,0:T(8,128)(2,1)}) %all-gather.14.cloned.1.call-update) | async-done | bytes 4194320 | tf_op jit(solution)/shard_map/all_gather | solution.py:53
  560.7 27.2 %fusion.93 = (f32[2048]{0:T(1024)}, bf16[2048,2048]{1,0:T(8,128)(2,1)S(1)}, bf16[2048,2048]{1,0:T(8,128)(2,1)}) fusion(f32[2048,2048]{1,0:T(8,128)} %fusion.104, f32[2048]{0:T(1024)S(1)} %copy-done.35, bf16[2048,1024]{1,0:T(8,128)(2,1)} %all-gather.14.cloned.1.call-done, bf16[1024,2048]{1,0:T(8,128)(2,1)} %bitcast.226), kind=kOutput, calls=%fused_computation.145 | convolution fusion | flops 8690595840 | bytes 41959424 | tf_op jit(solution)/shard_map/dot_general | solution.py:163
  591.2 11.2 fusion.84
  602.5 13.8 %convolution_convert_fusion.2 = bf16[2048,1024]{1,0:T(8,128)(2,1)} fusion(bf16[2048,2048]{1,0:T(8,128)(2,1)} %get-tuple-element.304, bf16[2048,1024]{1,0:T(8,128)(2,1)} %all-gather.16.cloned.1.call-done), kind=kOutput, calls=%fused_computation.124 | convolution fusion | flops 8592031744 | bytes 16777216 | tf_op jit(solution)/shard_map/dot_general | solution.py:166
  616.3 40.5 %reduce-scatter.13.cloned.1.call-done = bf16[2048,512]{1,0:T(8,128)(2,1)} async-done(((bf16[2048,1024]{1,0:T(8,128)(2,1)}), bf16[2048,512]{1,0:T(8,128)(2,1)}) %reduce-scatter.13.cloned.1.call-update) | async-done | bytes 2097168 | tf_op jit(solution)/shard_map/reduce_scatter | solution.py:57
  668.6 45.5 %reduce-scatter.11.cloned.1.call-done = bf16[2048,512]{1,0:T(8,128)(2,1)} async-done(((bf16[2048,1024]{1,0:T(8,128)(2,1)}), bf16[2048,512]{1,0:T(8,128)(2,1)}) %reduce-scatter.11.cloned.1.call-update) | async-done | bytes 2097168 | tf_op jit(solution)/shard_map/reduce_scatter | solution.py:169
  726.1 14.2 %fusion.87 = bf16[1024,2048]{1,0:T(8,128)(2,1)} fusion(bf16[2048,1024]{1,0:T(8,128)(2,1)} %all-gather.14.cloned.1.call-done, bf16[2048,2048]{1,0:T(8,128)(2,1)} %copy-done.38), kind=kOutput, calls=%fused_computation.123 | convolution fusion | flops 8592031744 | bytes 16777216 | tf_op jit(solution)/shard_map/td,tf->df/dot_general | solution.py:180
  740.4 14.0 %convolution_convert_fusion.3 = bf16[2048,1024]{1,0:T(8,128)(2,1)} fusion(bf16[2048,2048]{1,0:T(8,128)(2,1)} %get-tuple-element.304, bf16[2048,1024]{1,0:T(8,128)(2,1)} %all-gather.18.cloned.1.call-done), kind=kOutput, calls=%fused_computation.125 | convolution fusion | flops 8592031744 | bytes 16777216 | tf_op jit(solution)/shard_map/tf,td->fd/dot_general | solution.py:176
  754.5 28.5 %all-gather.20.cloned.1.call-done = bf16[2048,1024]{1,0:T(8,128)(2,1)} async-done(((bf16[2048,512]{1,0:T(8,128)(2,1)}), bf16[2048,1024]{1,0:T(8,128)(2,1)}) %all-gather.20.cloned.1.call-update) | async-done | bytes 4194320 | tf_op jit(solution)/shard_map/all_gather | solution.py:186
  802.2 125.7 %while.31 = (s32[]{:T(128)}, f32[4,512,8,64]{1,3,2,0:T(8,128)}, bf16[4,512,8,64]{1,3,2,0:T(8,128)(2,1)}, f32[4,512,8,64]{1,3,2,0:T(8,128)}, bf16[4,512,8,64]{1,3...) while((s32[]{:T(128)}, f32[4,512,8,64]{1,3,2,0:T(8,128)}, ...), condition=%wide.region_21.22_spmd.clone.clone, body=%wide.region_19.21_spmd.clone.sunk.clone | while | flops 1366815232 | bytes 156326224 | solution.py:192
  807.0 8.7 multiply_reduce_fusion.4
  838.4 8.7 multiply_reduce_fusion.4
  869.9 8.8 multiply_reduce_fusion.4
  901.3 8.7 multiply_reduce_fusion.4
  936.3 8.3 copy.58
  952.9 8.4 convolution_convert_fusion
  961.4 10.9 reduce-scatter.19.cloned.1.call-done
  972.3 61.7 %reduce-scatter.17.cloned.1.call-done = bf16[256,1536]{1,0:T(8,128)(2,1)} async-done(((bf16[1024,1536]{1,0:T(8,128)(2,1)}), bf16[256,1536]{1,0:T(8,128)(2,1)}) %reduce-scatter.17.cloned.1.call-update) | async-done | bytes 786448 | tf_op jit(solution)/shard_map/reduce_scatter | solution.py:226
  1034.0 11.7 convolution_convert_fusion.1
  1053.8 51.7 %all-reduce.8.cloned.1.call-done = (bf16[256,1536]{1,0:T(8,128)(2,1)}, bf16[512,256]{1,0:T(8,128)(2,1)}, bf16[256,2048]{1,0:T(8,128)(2,1)}, bf16[2048,256]{1,0:T(8,128)(2,1)}) async-done(((bf16[256,1536]{1,0:T(8,128)(2,1)}, bf16[512,256]{1,0:T(8,128)(2,1)}, bf16[256,2048]{1,0:T(8,128)(2,1)}, bf16[2048,256]{1,0:T(8,128)(2,1)}), (bf16[256,1536]{1,0:T(8,128)(2,1)}, bf16[512,256]{1,0:T(8,128)(2,1)}, ...) | async-done | bytes 3145744 | tf_op jit(solution)/shard_map/psum | solution.py:220
  1113.2 48.8 %reduce-scatter.15.cloned.1.call-done = bf16[2048,512]{1,0:T(8,128)(2,1)} async-done(((bf16[2048,1024]{1,0:T(8,128)(2,1)}), bf16[2048,512]{1,0:T(8,128)(2,1)}) %reduce-scatter.15.cloned.1.call-update) | async-done | bytes 2097168 | tf_op jit(solution)/shard_map/reduce_scatter | solution.py:57
  1184.2 59.9 %all-reduce = (f32[512]{0:T(512)}, f32[512]{0:T(512)}, f32[512]{0:T(512)}, f32[512]{0:T(512)}, f32[512]{0:T(512)}, /*index=5*/f32[512]{0:T(512)}, f32[512]{0:T(512)}, f32[2048]{0:T(1024)}, f32[512]{0:T(512)}) all-reduce(f32[512]{0:T(512)S(1)} %get-tuple-element.228, ...), channel_id=1, replica_groups=mesh['dp'=4,'row'=4,'col'=2] {'dp','row'}, use_global_device_ids=true, to_apply=%region_28.29 | all-reduce | flops 6144 | bytes 49152 | tf_op jit(solution)/shard_map/psum | solution.py:204
  (283 shorter events, 350.1 us)
Async XLA Ops:
  7.2 81.4 %all-gather.8.cloned.1.call-start = ((), (), s32[]{:S(2)}) async-start(), calls=%async_computation.8 | async-start | bytes 6291456 | tf_op jit(solution)/shard_map/all_gather | solution.py:53
  12.6 15.2 %copy-start.27 = (f32[512]{0:T(512)S(1)}, f32[512]{0:T(512)}, u32[]{:S(2)}) copy-start(f32[512]{0:T(512)} %param.23) | copy-start | bytes 6148
  31.5 122.2 %all-gather.10.cloned.1.call-start = ((), (), s32[]{:S(2)}) async-start(), calls=%async_computation.9 | async-start | bytes 3932160 | tf_op jit(solution)/shard_map/all_gather | solution.py:131
  32.2 225.5 %all-gather.12.cloned.1.call-start = ((), (), s32[]{:S(2)}) async-start(), calls=%async_computation.10 | async-start | bytes 1310720 | tf_op jit(solution)/shard_map/all_gather | solution.py:133
  32.9 330.2 %reduce-scatter.9.cloned.1.call-start = ((), (), s32[]{:S(2)}) async-start(), calls=%async_computation.11 | async-start | bytes 12582912 | tf_op jit(solution)/shard_map/reduce_scatter | solution.py:154
  33.2 130.3 %copy-start.4 = (bf16[4,512,8,64]{1,3,2,0:T(8,128)(2,1)}, bf16[4,512,8,64]{1,3,2,0:T(8,128)(2,1)S(1)}, u32[]{:S(2)}) copy-start(bf16[4,512,8,64]{1,3,2,0:T(8,128)(2,1)S(1)} %fusion.101) | copy-start | bytes 6291460
  265.2 171.3 %all-gather.18.cloned.1.call-start = ((), (), s32[]{:S(2)}) async-start(), calls=%async_computation.15 | async-start | bytes 6291456 | tf_op jit(solution)/shard_map/all_gather | solution.py:175
  270.6 92.5 %copy-start.32 = (f32[512]{0:T(512)S(1)}, f32[512]{0:T(512)}, u32[]{:S(2)}) copy-start(f32[512]{0:T(512)} %param.28) | copy-start | bytes 6148
  274.5 229.6 %all-gather.16.cloned.1.call-start = ((), (), s32[]{:S(2)}) async-start(), calls=%async_computation.13 | async-start | bytes 5242880 | tf_op jit(solution)/shard_map/all_gather | solution.py:134
  275.1 101.1 %copy-start.20 = (f32[512]{0:T(512)S(1)}, f32[512]{0:T(512)}, u32[]{:S(2)}) copy-start(f32[512]{0:T(512)} %param.29) | copy-start | bytes 6148
  275.1 101.1 %copy-start.28 = (f32[512]{0:T(512)S(1)}, f32[512]{0:T(512)}, u32[]{:S(2)}) copy-start(f32[512]{0:T(512)} %param.30) | copy-start | bytes 6148
  275.1 285.6 %all-gather.14.cloned.1.call-start = ((), (), s32[]{:S(2)}) async-start(), calls=%async_computation.12 | async-start | bytes 6291456 | tf_op jit(solution)/shard_map/all_gather | solution.py:53
  275.2 108.7 %collective-permute-start = (bf16[256,2048]{1,0:T(8,128)(2,1)S(1)}, bf16[256,2048]{1,0:T(8,128)(2,1)S(1)}, u32[]{:S(2)}, u32[]{:S(2)}) collective-permute-start(bf16[256,2048]{1,0:T(8,128)(2,1)S(1)} %copy-done.13), channel_id=1, source_target_pairs={{0,2},{2,4},{4,6},{6,0},{1,3},{3,5},{5,7},{7,1},{8,10},{10,12},{12... | collective-permute-start | bytes 3145736 | tf_op jit(solution)/shard_map/ppermute | solution.py:26
  380.2 276.7 %reduce-scatter.13.cloned.1.call-start = ((), (), s32[]{:S(2)}) async-start(), calls=%async_computation.16 | async-start | bytes 6291456 | tf_op jit(solution)/shard_map/reduce_scatter | solution.py:57
  380.3 27.2 %collective-permute-start.2 = (bf16[256,2048]{1,0:T(8,128)(2,1)S(1)}, bf16[256,2048]{1,0:T(8,128)(2,1)S(1)}, u32[]{:S(2)}, u32[]{:S(2)}) collective-permute-start(bf16[256,2048]{1,0:T(8,128)(2,1)S(1)} %copy-done.13), channel_id=1, source_target_pairs={{2,0},{4,2},{6,4},{0,6},{3,1},{5,3},{7,5},{1,7},{10,8},{12,10},{14... | collective-permute-start | bytes 3145736 | tf_op jit(solution)/shard_map/ppermute | solution.py:28
  383.9 44.0 %collective-permute-start.1 = (bf16[256,2048]{1,0:T(8,128)(2,1)S(1)}, bf16[256,2048]{1,0:T(8,128)(2,1)}, u32[]{:S(2)}, u32[]{:S(2)}) collective-permute-start(bf16[256,2048]{1,0:T(8,128)(2,1)S(1)} %collective-permute-done), channel_id=1, source_target_pairs={{0,2},{2,4},{4,6},{6,0},{1,3},{3,5},{5,7},{7,1},{8,10},{10,12},{12... | collective-permute-start | bytes 3145736 | tf_op jit(solution)/shard_map/ppermute | solution.py:26
  436.4 124.3 %copy-start.35 = (f32[2048]{0:T(1024)S(1)}, f32[2048]{0:T(1024)}, u32[]{:S(2)}) copy-start(f32[2048]{0:T(1024)} %param.32) | copy-start | bytes 24580
  560.7 30.4 %copy-start.12 = (bf16[4,256,2048]{2,1,0:T(8,128)(2,1)S(1)}, bf16[4,256,2048]{2,1,0:T(8,128)(2,1)}, u32[]{:S(2)}) copy-start(bf16[4,256,2048]{2,1,0:T(8,128)(2,1)} %gather_fusion) | copy-start | bytes 12582916
  602.4 111.8 %reduce-scatter.11.cloned.1.call-start = ((), (), s32[]{:S(2)}) async-start(), calls=%async_computation.14 | async-start | bytes 6291456 | tf_op jit(solution)/shard_map/reduce_scatter | solution.py:169
  616.3 97.9 %copy-start.29 = (f32[512]{0:T(512)S(1)}, f32[512]{0:T(512)}, u32[]{:S(2)}) copy-start(f32[512]{0:T(512)} %param.34) | copy-start | bytes 6148
  616.3 166.7 %all-gather.20.cloned.1.call-start = ((), (), s32[]{:S(2)}) async-start(), calls=%async_computation.17 | async-start | bytes 6291456 | tf_op jit(solution)/shard_map/all_gather | solution.py:186
  656.9 57.3 %copy-start.8 = (bf16[2048,512]{1,0:T(8,128)(2,1)S(1)}, bf16[2048,512]{1,0:T(8,128)(2,1)}, u32[]{:S(2)}) copy-start(bf16[2048,512]{1,0:T(8,128)(2,1)} %reduce-scatter.13.cloned.1.call-done) | copy-start | bytes 6291460
  726.1 235.3 %reduce-scatter.21.cloned.1.call-start = ((), (), s32[]{:S(2)}) async-start(), calls=%async_computation.21 | async-start | bytes 5242880 | tf_op jit(solution)/shard_map/reduce_scatter | solution.py:229
  740.3 221.1 %reduce-scatter.23.cloned.1.call-start = ((), (), s32[]{:S(2)}) async-start(), calls=%async_computation.22 | async-start | bytes 5242880 | tf_op jit(solution)/shard_map/reduce_scatter | solution.py:235
  754.4 28.6 %copy-start.34 = (bf16[512,1024]{1,0:T(8,128)(2,1)S(1)}, bf16[512,1024]{1,0:T(8,128)(2,1)}, u32[]{:S(2)}) copy-start(bf16[512,1024]{1,0:T(8,128)(2,1)} %all-gather.12.cloned.1.call-done) | copy-start | bytes 3145732
  754.4 217.9 %reduce-scatter.19.cloned.1.call-start = ((), (), s32[]{:S(2)}) async-start(), calls=%async_computation.20 | async-start | bytes 1310720 | tf_op jit(solution)/shard_map/reduce_scatter | solution.py:232
  928.0 106.0 %reduce-scatter.17.cloned.1.call-start = ((), (), s32[]{:S(2)}) async-start(), calls=%async_computation.19 | async-start | bytes 3932160 | tf_op jit(solution)/shard_map/reduce_scatter | solution.py:226
  961.3 144.1 %all-reduce.8.cloned.1.call-start = ((), (), s32[]{:S(2)}) async-start(), calls=%async_computation.23 | async-start | bytes 6291456 | tf_op jit(solution)/shard_map/psum | solution.py:220
  1034.0 128.0 %reduce-scatter.15.cloned.1.call-start = ((), (), s32[]{:S(2)}) async-start(), calls=%async_computation.18 | async-start | bytes 6291456 | tf_op jit(solution)/shard_map/reduce_scatter | solution.py:57
  1105.5 56.6 %copy-start.17 = (f32[2048]{0:T(1024)S(1)}, f32[2048]{0:T(1024)}, u32[]{:S(2)}) copy-start(f32[2048]{0:T(1024)} %copy-done.16) | copy-start | bytes 24580
  1105.5 56.6 %copy-start.19 = (f32[2048]{0:T(1024)S(1)}, f32[2048]{0:T(1024)}, u32[]{:S(2)}) copy-start(f32[2048]{0:T(1024)} %copy-done.18) | copy-start | bytes 24580
  1105.5 56.6 %copy-start.22 = (f32[512]{0:T(512)S(1)}, f32[512]{0:T(512)}, u32[]{:S(2)}) copy-start(f32[512]{0:T(512)} %param.22) | copy-start | bytes 6148
  (38 other events, 208.1 us)
Sparse Core Ops, SparseCore 0:
  31.6 56.9 all-gather.7
  90.2 63.4 all-gather.9
  155.3 28.8 all-gather.11
  265.3 97.8 reduce-scatter.8
  365.2 56.7 all-gather.17
  423.5 80.6 all-gather.15
  505.8 54.9 all-gather.13
  602.5 54.3 reduce-scatter.12
  659.8 54.3 reduce-scatter.10
  726.2 56.7 all-gather.19
  785.4 76.7 reduce-scatter.20
  864.3 77.2 reduce-scatter.22
  944.6 27.6 reduce-scatter.18
  975.0 58.8 reduce-scatter.16
  1036.4 68.9 all-reduce.7
  1107.6 54.3 reduce-scatter.14
